TPU v7x, 32 devices: a whole 2x2x4 slice. The times are simulated.
32 devices in a mesh: grp: 2 (over x), bits: 16 (over z, y, core).
Axes of the slice: x: 2, y: 2, z: 4, core: 2. Of those that a mesh axis runs over, the one named last changes fastest.
Arguments:
- prefix: bfloat16 [128, 16, 1024], P(('grp', 'bits')), parts along dimension 0, may hold values from -6 to 6
- first_suffix: bfloat16 [8, 2, 512, 512], P('grp', None, 'bits'), parts along dimension 0, may hold values from -0.109375 to 0.109375
- pair_prefix: int32 [256, 3], P(('grp', 'bits')), parts along dimension 0, may hold values from 0 to 3
- pair_suffix: int32 [256, 3], P(('grp', 'bits')), parts along dimension 0, may hold values from 0 to 3, all different within a row
- merge_count: int32 [256], P(('grp', 'bits')), parts along dimension 0, may hold values from 1 to 3, as said below
- suffix: bfloat16 [32, 2, 512, 512], P(('grp', 'bits')), parts along dimension 0, may hold values from -0.1875 to 0.1875
- routes: int32 [256, 12], P(('grp', 'bits')), parts along dimension 0, may hold values from 0 to 15, all different within a row; in each aligned block of 8 rows (0 to 7, 8 to 15, ...) at most 8 rows name the same one
- cap: bfloat16 [2, 512, 64], replicated, may hold values from -0.0546875 to 0.0546875
Outputs:
- capped: float32 [256, 16, 128], P(('grp', 'bits')), parts along dimension 0
There are 2 independent parts, one for each index of `grp`. A program takes and returns all parts, laid end to end along the dimension named above; an argument that names none is the same for every part. Nothing has to cross between parts.
Inputs may be any that keep to these rules, and one draw needn't show every extreme that they name: `pair_suffix`: each row names 3 different lifetime-one blocks. `merge_count`: some piece has exactly 3 merges and some exactly one. `routes`: each row names 12 different suffixes; in each aligned block of 8 rows no suffix is named by more than 8 rows, a bound that some block reaches.
All inputs are finite; a program needn't handle non-finite values.
Results may differ from a plain program's by a relative error of at most 0.005.
Values may be sent and summed in bfloat16 or wider, within the bound.
A program may use at most 64 MiB of HBM per device.

v0:
```python
import jax
import jax.numpy as jnp
from jax import lax
from jax.sharding import PartitionSpec as P

HIGHEST_PRECISION = lax.Precision.HIGHEST


def complex_form(blocks):
    real_part = blocks[..., 0, :, :]
    imag_part = blocks[..., 1, :, :]
    upper_half = jnp.concatenate([real_part, imag_part], axis=-1)
    lower_half = jnp.concatenate([-imag_part, real_part], axis=-1)
    return jnp.concatenate([upper_half, lower_half], axis=-2)


def on_device(prefix, first_suffix, pair_prefix, pair_suffix, merge_count, suffix, routes, cap):
    pieces = pair_prefix.shape[0]
    merges = pair_prefix.shape[1]
    held_blocks = prefix.shape[0]
    rows_piece = prefix.shape[1]
    twice_width = prefix.shape[2]
    half_width = twice_width // 2
    first_count = first_suffix.shape[0]
    listed = routes.shape[1]
    owners = lax.axis_size("bits")
    slot_count = min(pieces, max(2, (2 * pieces * listed + owners - 1) // owners))
    live_mask = lax.broadcasted_iota(jnp.int32, (pieces, merges), 1) < merge_count[:, None]
    matches = (
        pair_suffix[:, :, None] == lax.broadcasted_iota(jnp.int32, (pieces, merges, first_count), 2)
    ) & live_mask[:, :, None]
    which_block = pair_prefix[:, :, None] == lax.broadcasted_iota(
        jnp.int32, (pieces, merges, held_blocks), 2
    )
    prefix_picks = jnp.einsum(
        "ika,ikp->iap", matches.astype(jnp.float32), which_block.astype(jnp.float32)
    ).astype(jnp.bfloat16)
    selected = jnp.einsum(
        "iap,prc->airc", prefix_picks, prefix, preferred_element_type=jnp.float32
    ).astype(jnp.bfloat16)
    selected = selected.reshape(first_count, pieces * rows_piece, twice_width)
    portion = lax.all_gather(first_suffix, "bits", axis=2, tiled=True)
    count_rows = portion.shape[2]
    real_cols = lax.slice_in_dim(selected, 0, count_rows, axis=2)
    imag_cols = lax.dynamic_slice_in_dim(selected, half_width, count_rows, 2)
    left_side = jnp.concatenate([real_cols, imag_cols], axis=2)
    upper_half = jnp.concatenate([portion[:, 0], portion[:, 1]], axis=2)
    lower_half = jnp.concatenate([-portion[:, 1], portion[:, 0]], axis=2)
    right_side = jnp.concatenate([upper_half, lower_half], axis=1)
    state_rows = jnp.einsum(
        "arc,acw->rw", left_side, right_side, preferred_element_type=jnp.float32
    )
    state_rows = state_rows.astype(jnp.bfloat16).reshape(pieces, rows_piece, twice_width)
    named_by = jnp.sum(
        (routes[:, :, None] == lax.broadcasted_iota(jnp.int32, (pieces, listed, owners), 2)).astype(
            jnp.int32
        ),
        axis=1,
    )
    slot_rank = jnp.cumsum(named_by, axis=0) - named_by
    slot_hit = (
        slot_rank[:, :, None] == lax.broadcasted_iota(jnp.int32, (pieces, owners, slot_count), 2)
    ) & (named_by[:, :, None] > 0)
    dispatch = jnp.transpose(slot_hit, (1, 2, 0)).astype(jnp.bfloat16)
    outgoing = jnp.einsum(
        "dmi,irc->dmrc", dispatch, state_rows, preferred_element_type=jnp.float32
    ).astype(jnp.bfloat16)
    own_form = complex_form(suffix[0])
    cap_form = complex_form(cap)
    products = jnp.einsum(
        "smrc,cw->smrw",
        lax.all_to_all(outgoing, "bits", split_axis=0, concat_axis=0, tiled=True),
        own_form,
        preferred_element_type=jnp.float32,
    ).astype(jnp.bfloat16)
    capped_terms = jnp.einsum(
        "smrw,wv->smrv", products, cap_form, preferred_element_type=jnp.float32
    )
    returned = lax.all_to_all(
        capped_terms.astype(jnp.bfloat16), "bits", split_axis=0, concat_axis=0, tiled=True
    ).astype(capped_terms.dtype)
    return jnp.einsum(
        "dmi,dmrv->irv", dispatch.astype(jnp.float32), returned, precision=HIGHEST_PRECISION
    )


def solution(mesh):
    return jax.shard_map(
        on_device,
        mesh=mesh,
        in_specs=(
            P(("grp", "bits"), None, None),
            P("grp", None, "bits", None),
            P(("grp", "bits"), None),
            P(("grp", "bits"), None),
            P(("grp", "bits")),
            P(("grp", "bits"), None, None, None),
            P(("grp", "bits"), None),
            P(),
        ),
        out_specs=P(("grp", "bits"), None, None),
        check_vma=False,
    )
```

profile of v0, /device:TPU:0, one launch (start us, length us, event | category | flops | bytes accessed | tf_op | source)
XLA Modules:
  0.0 205.2 jit_solution(14975206516049845053)
XLA Ops:
  6.5 0.0 all-gather.2.cloned.1.call-start
  6.5 1.7 copy.52
  8.2 0.0 all-gather.2.cloned.1.call-update
  8.2 0.8 copy.47
  9.0 0.8 copy.48
  9.7 0.7 iota_compare_fusion.5
  10.5 0.2 fusion.32
  10.7 1.3 fusion.22
  12.0 0.6 copy.51
  12.6 0.8 copy.46
  13.3 0.1 convert_reduce_fusion
  13.5 49.2 %all-gather.2.cloned.1.call-done = bf16[4,2,512,512]{3,2,0,1:T(8,128)(2,1)} async-done(((bf16[4,2,32,512]{3,2,0,1:T(8,128)(2,1)}), bf16[4,2,512,512]{3,2,0,1:T(8,128)(2,1)}) %all-gather.2.cloned.1.call-update) | async-done | bytes 4194320 | tf_op jit(solution)/shard_map/all_gather | solution.py:42
  62.7 0.0 copy-start
  62.7 2.7 %slice_bitcast_fusion = (bf16[4,512,512]{2,1,0:T(8,128)(2,1)S(1)}, bf16[4,512,512]{2,1,0:T(8,128)(2,1)S(1)}) fusion(bf16[4,2,512,512]{3,2,0,1:T(8,128)(2,1)} %all-gather.2.cloned.1.call-done), kind=kLoop, calls=%fused_computation.11 | loop fusion | bytes 8388608 | tf_op jit(solution)/shard_map/squeeze | solution.py:47
  65.3 0.8 copy-done
  66.1 0.1 fusion.63
  66.3 1.3 fusion.29
  67.6 1.6 convolution_convert_fusion
  69.1 4.3 %copy.54 = bf16[16,8,16,1024]{3,2,1,0:T(8,128)(2,1)} copy(bf16[16,8,16,1024]{3,0,2,1:T(8,128)(2,1)S(1)} %convolution_convert_fusion) | data formatting | bytes 8388608 | tf_op jit(solution)/shard_map/convert_element_type | solution.py:67
  73.4 0.0 copy-start.2
  73.4 0.0 copy-start.1
  73.4 4.9 %all-to-all-start = ((bf16[16,8,16,1024]{3,2,1,0:T(8,128)(2,1)}), bf16[16,8,16,1024]{3,2,1,0:T(8,128)(2,1)}, u32[]{:S(2)}, u32[]{:S(2)}) async-start(bf16[16,8,16,1024]{3,2,1,0:T(8,128)(2,1)} %copy.54), calls=%async_computation | async-start | bytes 8388608 | tf_op jit(solution)/shard_map/all_to_all | solution.py:72
  78.3 0.0 copy-done.2
  78.3 0.1 copy.68
  78.5 0.1 copy.67
  78.6 0.0 copy-done.1
  78.7 0.1 slice_bitcast_fusion.2
  78.7 76.9 %all-to-all-done = bf16[16,8,16,1024]{3,2,1,0:T(8,128)(2,1)} async-done(((bf16[16,8,16,1024]{3,2,1,0:T(8,128)(2,1)}), bf16[16,8,16,1024]{3,2,1,0:T(8,128)(2,1)}, u32[]{:S(2)}, u32[]{:S(2)}) %all-to-all-start) | async-done | bytes 4194336 | tf_op jit(solution)/shard_map/all_to_all | solution.py:72
  155.6 7.9 %fusion.23 = bf16[16,8,16,128]{3,2,1,0:T(8,128)(2,1)S(1)} fusion(bf16[16,8,16,1024]{3,2,1,0:T(8,128)(2,1)} %all-to-all-done, bf16[512,512]{1,0:T(8,128)(2,1)S(1)} %get-tuple-element.8, bf16[512,512]{1,0:T(8,128)(2,1)S(1)} %fusion.62, bf16[512,512]{1,0:T(8,128)(2,1)S(1)} %get-tuple-element.7, bf16[512,64]{1,0:T(8,128)(2,1)S(1)} %bitcast.66, ...), kind=kOutput, calls=%fused_computation.23 | convolution fusion | flops 4843634688 | bytes 6488064 | tf_op jit(solution)/shard_map/smrw,wv->smrv/dot_general | solution.py:76
  163.5 0.1 copy.57
  163.7 33.7 %all_to_all.10 = bf16[16,8,16,128]{3,1,2,0:T(8,128)(2,1)S(1)} all-to-all(bf16[16,8,16,128]{3,1,2,0:T(8,128)(2,1)S(1)} %copy.57), channel_id=1, replica_groups=mesh['grp'=2,'bits'=16] {'bits'}, dimensions={0} | all-to-all | bytes 1048576 | tf_op jit(solution)/shard_map/all_to_all | solution.py:79
  197.4 0.4 convolution_bitcast_fusion
  197.8 0.6 copy.59
  (6 shorter events, 0.1 us)
Async XLA Ops:
  6.5 56.1 %all-gather.2.cloned.1.call-start = ((), (), s32[]{:S(2)}) async-start(), calls=%async_computation.2 | async-start | bytes 4456448 | tf_op jit(solution)/shard_map/all_gather | solution.py:42
  62.7 3.4 %copy-start = (bf16[4,2,512,512]{3,2,0,1:T(8,128)(2,1)S(1)}, bf16[4,2,512,512]{3,2,0,1:T(8,128)(2,1)}, u32[]{:S(2)}) copy-start(bf16[4,2,512,512]{3,2,0,1:T(8,128)(2,1)} %all-gather.2.cloned.1.call-done) | copy-start | bytes 12582916
  73.4 4.9 %copy-start.2 = (bf16[2,512,64]{1,2,0:T(8,128)(2,1)S(1)}, bf16[2,512,64]{1,2,0:T(8,128)(2,1)}, u32[]{:S(2)}) copy-start(bf16[2,512,64]{1,2,0:T(8,128)(2,1)} %param.15) | copy-start | bytes 393220
  73.4 5.2 %copy-start.1 = (bf16[1,2,512,512]{3,2,1,0:T(8,128)(2,1)S(1)}, bf16[1,2,512,512]{3,2,1,0:T(8,128)(2,1)}, u32[]{:S(2)}) copy-start(bf16[1,2,512,512]{3,2,1,0:T(8,128)(2,1)} %param.13) | copy-start | bytes 3145732
  73.4 82.2 %all-to-all-start = ((bf16[16,8,16,1024]{3,2,1,0:T(8,128)(2,1)}), bf16[16,8,16,1024]{3,2,1,0:T(8,128)(2,1)}, u32[]{:S(2)}, u32[]{:S(2)}) async-start(bf16[16,8,16,1024]{3,2,1,0:T(8,128)(2,1)} %copy.54), calls=%async_computation | async-start | bytes 8388608 | tf_op jit(solution)/shard_map/all_to_all | solution.py:72
Sparse Core Ops, SparseCore 0:
  9.5 53.1 all-gather.1
where the time goes:
time: 206 us; the launch traced here: 205 us
  waiting for transfers between devices  126 us (61%)
  blocking collectives  33.7 us (16%)
  between operations  13.5 us (7%)
  local copies, waits for them, and re-layouts  13.4 us (7%)
  matrix products  12.7 us (6%)
  starting transfers between devices  4.85 us (2%)
    all_to_all x1, waiting for transfers between devices, on_device(): lax.all_to_all(outgoing, 'bits', split_axis=0, concat_axis=0, tiled=True)  76.9 us
    all_gather x1, waiting for transfers between devices, on_device(): portion = lax.all_gather(first_suffix, 'bits', axis=2, tiled=True)  49.2 us
    all_to_all x1, blocking collectives, on_device(): lax.all_to_all(capped_terms.astype(jnp.bfloat16), 'bits', split_axis=0, c...  33.7 us
    dot_general x1, matrix products, on_device(): jnp.einsum('smrw,wv->smrv', products, cap_form, preferred_element_type=jn...  7.92 us
    unnamed x12, local copies, waits for them, and re-layouts  4.98 us
    all_to_all x1, starting transfers between devices, on_device(): lax.all_to_all(outgoing, 'bits', split_axis=0, concat_axis=0, tiled=True)  4.85 us
    convert_element_type x1, local copies, waits for them, and re-layouts, on_device(): outgoing = jnp.einsum('dmi,irc->dmrc', dispatch, state_rows, preferred_el...  4.3 us
  transfers between devices with their start and end apart: 2, of which 2 were waited for; matrix products, arithmetic and copies ran while one was open for 3% of the time, Pallas kernels for 0%

commit v1 on v0

--- a/solution.py
+++ b/solution.py
@@ -14,7 +14,7 @@
     return jnp.concatenate([upper_half, lower_half], axis=-2)
 
 
-def on_device(prefix, first_suffix, pair_prefix, pair_suffix, merge_count, suffix, routes, cap):
+def on_device_sparse(prefix, first_suffix, pair_prefix, pair_suffix, merge_count, suffix, routes, cap):
     pieces = pair_prefix.shape[0]
     merges = pair_prefix.shape[1]
     held_blocks = prefix.shape[0]
@@ -84,6 +84,80 @@
     )
 
 
+def weights_of(pair_prefix, pair_suffix, merge_count, held_blocks, first_count):
+    pieces, merges = pair_prefix.shape
+    live_mask = lax.broadcasted_iota(jnp.int32, (pieces, merges), 1) < merge_count[:, None]
+    matches = (
+        pair_suffix[:, :, None] == lax.broadcasted_iota(jnp.int32, (pieces, merges, first_count), 2)
+    ) & live_mask[:, :, None]
+    which_block = pair_prefix[:, :, None] == lax.broadcasted_iota(
+        jnp.int32, (pieces, merges, held_blocks), 2
+    )
+    return jnp.sum(
+        (matches[:, :, :, None] & which_block[:, :, None, :]).astype(jnp.float32), axis=1
+    ).astype(jnp.bfloat16)
+
+
+def on_device_dense(prefix, first_suffix, pair_prefix, pair_suffix, merge_count, suffix, routes, cap):
+    pieces = pair_prefix.shape[0]
+    held_blocks, rows_piece, twice_width = prefix.shape
+    first_count = first_suffix.shape[0]
+    owners = lax.axis_size("bits")
+    listed = routes.shape[1]
+    portion = lax.all_gather(first_suffix, "bits", axis=2, tiled=True)
+    cap_form = jnp.concatenate([cap[0], cap[1]], axis=1)
+    cap_turn = jnp.concatenate([-cap[1], cap[0]], axis=1)
+    closed = (
+        jnp.dot(suffix[0, 0], cap_form, preferred_element_type=jnp.float32)
+        + jnp.dot(suffix[0, 1], cap_turn, preferred_element_type=jnp.float32)
+    ).astype(jnp.bfloat16)
+    closed_all = lax.all_gather(closed, "bits", axis=1, tiled=False)
+    picks = weights_of(pair_prefix, pair_suffix, merge_count, held_blocks, first_count)
+    selected = jnp.einsum(
+        "iap,prc->airc", picks, prefix, preferred_element_type=jnp.float32
+    ).astype(jnp.bfloat16)
+    selected = selected.reshape(first_count, pieces * rows_piece, twice_width)
+    half = twice_width // 2
+    real = selected[:, :, :half]
+    imag = selected[:, :, half:]
+    by_real = jnp.einsum(
+        "arc,acw->rw", jnp.concatenate([real, -imag], axis=2),
+        portion.reshape(first_count, twice_width, half), preferred_element_type=jnp.float32,
+    )
+    by_imag = jnp.einsum(
+        "arc,acw->rw", jnp.concatenate([imag, real], axis=2),
+        portion.reshape(first_count, twice_width, half), preferred_element_type=jnp.float32,
+    )
+    state_real = by_real.astype(jnp.bfloat16)
+    state_imag = by_imag.astype(jnp.bfloat16)
+    flat = closed_all.reshape(half, -1)
+    capw = cap.shape[2]
+    stacked = jnp.concatenate([state_real, state_imag], axis=0)
+    both = jnp.dot(stacked, flat, preferred_element_type=jnp.float32)
+    both = both.reshape(2, pieces, rows_piece, owners, 2, capw)
+    named = jnp.sum(
+        (routes[:, :, None] == lax.broadcasted_iota(jnp.int32, (pieces, listed, owners), 2)).astype(
+            jnp.float32
+        ),
+        axis=1,
+    )
+    summed = jnp.sum(both * named[None, :, None, :, None, None], axis=3)
+    out_real = summed[0, :, :, 0] - summed[1, :, :, 1]
+    out_imag = summed[0, :, :, 1] + summed[1, :, :, 0]
+    return jnp.concatenate([out_real, out_imag], axis=-1)
+
+
+def on_device(prefix, first_suffix, pair_prefix, pair_suffix, merge_count, suffix, routes, cap):
+    pieces = pair_prefix.shape[0]
+    listed = routes.shape[1]
+    owners = lax.axis_size("bits")
+    slots = min(pieces, max(2, (2 * pieces * listed + owners - 1) // owners))
+    body = on_device_dense if slots == pieces else on_device_sparse
+    return body(
+        prefix, first_suffix, pair_prefix, pair_suffix, merge_count, suffix, routes, cap
+    )
+
+
 def solution(mesh):
     return jax.shard_map(
         on_device,

time: 206 us -> 116 us (0.56)
  waiting for transfers between devices: 126 us -> 87.5 us
  blocking collectives: 33.7 us -> 0 us
  local copies, waits for them, and re-layouts: 13.4 us -> 1.96 us
  starting transfers between devices: 4.85 us -> 0.07 us
  matrix products: 12.7 us -> 10.5 us
    all_to_all x1 -> x0, waiting for transfers between devices: 76.9 us -> none  [on_device(): lax.all_to_all(outgoing, 'bits', split_axis=0, concat_axis=0, tiled=True)]
    all_gather x1 -> x2, waiting for transfers between devices: 49.2 us -> 86.8 us  [the longest x1 48.8 us: on_device_dense(): portion = lax.all_gather(first_suffix, 'bits', axis=2, tiled=True)]
    all_to_all x1 -> x0, blocking collectives: 33.7 us -> none  [on_device(): lax.all_to_all(capped_terms.astype(jnp.bfloat16), 'bits', split_axis=0, c...]
    all_to_all x1 -> x0, starting transfers between devices: 4.85 us -> none  [on_device(): lax.all_to_all(outgoing, 'bits', split_axis=0, concat_axis=0, tiled=True)]
    unnamed x12 -> x13, local copies, waits for them, and re-layouts: 4.98 us -> 0.5 us
    convert_element_type x3 -> x1, local copies, waits for them, and re-layouts: 5.03 us -> 0.58 us  [on_device_dense(): selected = jnp.einsum('iap,prc->airc', picks, prefix, preferred_element_t...]
    dot_general x6, matrix products: 12.7 us -> 10.5 us  [the longest x1 3.04 us: on_device_dense(): jnp.einsum('arc,acw->rw', jnp.concatenate([real, -imag], axis=2), portion...]
  transfers between devices with their start and end apart: 2 -> 2, of which waited for: 2 -> 2; matrix products, arithmetic and copies ran while one was open for 3% -> 9% of each run, Pallas kernels for 0% -> 0%
where the time goes in v1:
time: 116 us; the launch traced here: 115 us
  waiting for transfers between devices  87.5 us (75%)
  between operations  13.6 us (12%)
  matrix products  10.5 us (9%)
  local copies, waits for them, and re-layouts  1.96 us (2%)
  other arithmetic  1.83 us (2%)
    all_gather x1, waiting for transfers between devices, on_device_dense(): portion = lax.all_gather(first_suffix, 'bits', axis=2, tiled=True)  48.8 us
    all_gather x1, waiting for transfers between devices, on_device_dense(): closed_all = lax.all_gather(closed, 'bits', axis=1, tiled=False)  38 us
    dot_general x1, matrix products, on_device_dense(): jnp.einsum('arc,acw->rw', jnp.concatenate([real, -imag], axis=2), portion...  3.04 us
    dot_general x1, matrix products, on_device_dense(): both = jnp.dot(stacked, flat, preferred_element_type=jnp.float32)  2.88 us
  transfers between devices with their start and end apart: 2, of which 2 were waited for; matrix products, arithmetic and copies ran while one was open for 9% of the time, Pallas kernels for 0%

profile of v1, /device:TPU:0, one launch (start us, length us, event | category | flops | bytes accessed | tf_op | source)
XLA Modules:
  0.0 115.4 jit_solution(9288397554373046558)
XLA Ops:
  6.5 0.0 copy-start.5
  6.5 0.0 copy-start.2
  6.5 0.0 copy-start.3
  6.5 0.0 copy-start
  6.5 0.0 all-gather.4.cloned.1.call-start
  6.6 0.7 all-gather.4.cloned.1.call-update
  7.3 0.0 all-gather.6.cloned.1.call-start
  7.3 0.8 fusion.34
  8.2 0.9 slice_bitcast_fusion.3
  9.1 1.3 %fusion.12 = f32[128,512]{1,0:T(8,128)S(1)} fusion(bf16[1,2,512,512]{3,2,1,0:T(8,128)(2,1)} %param.13, bf16[512,64]{0,1:T(8,128)(2,1)S(1)} %get-tuple-element.9, bf16[512,64]{0,1:T(8,128)(2,1)S(1)} %get-tuple-element.8), kind=kOutput, calls=%fused_computation.17 | convolution fusion | flops 67371008 | bytes 917504 | tf_op jit(solution)/shard_map/dot_general | solution.py:111
  10.4 0.0 copy-start.1
  10.4 2.0 %fusion.4 = bf16[512,128]{0,1:T(8,128)(2,1)} fusion(f32[128,512]{1,0:T(8,128)S(1)} %fusion.12, bf16[1,2,512,512]{3,2,1,0:T(8,128)(2,1)} %param.13, bf16[512,64]{0,1:T(8,128)(2,1)S(1)} %get-tuple-element.8, bf16[512,64]{0,1:T(8,128)(2,1)S(1)} %fusion.34), kind=kOutput, calls=%fused_computation.9 | convolution fusion | flops 67502080 | bytes 1048576 | tf_op jit(solution)/shard_map/dot_general | solution.py:112
  12.4 0.0 all-gather.6.cloned.1.call-update
  12.5 0.0 copy-done.5
  12.5 0.0 copy-done.2
  12.5 0.0 copy-done.3
  12.5 0.0 copy-done
  12.6 0.5 fusion
  13.0 0.6 copy.23
  13.6 0.0 copy-done.1
  13.6 0.1 copy.24
  13.7 0.1 convert_reduce_fusion
  13.8 0.1 slice_negate_fusion
  13.9 48.8 %all-gather.4.cloned.1.call-done = bf16[4,2,512,512]{3,2,1,0:T(8,128)(2,1)} async-done(((bf16[4,2,32,512]{3,2,1,0:T(8,128)(2,1)}), bf16[4,2,512,512]{3,2,1,0:T(8,128)(2,1)}) %all-gather.4.cloned.1.call-update) | async-done | bytes 4194320 | tf_op jit(solution)/shard_map/all_gather | solution.py:107
  62.7 0.0 copy-start.4
  62.7 3.0 %fusion.1 = bf16[128,512]{1,0:T(8,128)(2,1)S(1)} fusion(bf16[4,1024,512]{2,1,0:T(8,128)(2,1)} %bitcast.66, bf16[4,128,512]{2,1,0:T(8,128)(2,1)S(1)} %get-tuple-element.5, bf16[4,128,512]{2,1,0:T(8,128)(2,1)S(1)} %get-tuple-element.7), kind=kOutput, calls=%fused_computation.6 | convolution fusion | flops 539033600 | bytes 5373952 | tf_op jit(solution)/shard_map/arc,acw->rw/dot_general | solution.py:123
  65.7 0.4 copy-done.4
  66.1 0.7 fusion.2
  66.9 38.0 %all-gather.6.cloned.1.call-done = bf16[512,2048]{0,1:T(8,128)(2,1)} async-done(((bf16[512,128]{0,1:T(8,128)(2,1)}), bf16[512,2048]{0,1:T(8,128)(2,1)}) %all-gather.6.cloned.1.call-update) | async-done | bytes 2097168 | tf_op jit(solution)/shard_map/all_gather | solution.py:114
  104.9 2.9 %multiply_reduce_fusion = f32[2,8,16,2,64]{4,2,3,1,0:T(8,128)S(1)} fusion(bf16[2,8,16,512,1,1]{3,2,5,4,1,0:T(8,128)(2,1)S(1)} %bitcast.65, bf16[16,2,64,512,1,1]{3,2,1,0,5,4:T(8,128)(2,1)} %bitcast.68, f32[8,16]{1,0:T(8,128)S(1)} %convert_reduce_fusion), kind=kOutput, calls=%fused_computation | convolution fusion | flops 537886720 | bytes 2490880 | tf_op jit(solution)/shard_map/dot_general | solution.py:136
  107.9 0.7 pad_maximum_fusion.1
  (6 shorter events, 0.1 us)
Async XLA Ops:
  6.5 5.9 %copy-start.5 = (s32[8]{0:T(128)S(1)}, s32[8]{0:T(128)}, u32[]{:S(2)}) copy-start(s32[8]{0:T(128)} %param.12) | copy-start | bytes 100
  6.5 5.9 %copy-start.2 = (s32[8,3]{0,1:T(4,128)S(1)}, s32[8,3]{0,1:T(4,128)}, u32[]{:S(2)}) copy-start(s32[8,3]{0,1:T(4,128)} %param.10) | copy-start | bytes 292
  6.5 6.0 %copy-start.3 = (s32[8,3]{0,1:T(4,128)S(1)}, s32[8,3]{0,1:T(4,128)}, u32[]{:S(2)}) copy-start(s32[8,3]{0,1:T(4,128)} %param.11) | copy-start | bytes 292
  6.5 6.0 %copy-start = (bf16[4,16,1024]{2,1,0:T(8,128)(2,1)S(1)}, bf16[4,16,1024]{2,1,0:T(8,128)(2,1)}, u32[]{:S(2)}) copy-start(bf16[4,16,1024]{2,1,0:T(8,128)(2,1)} %param.8) | copy-start | bytes 393220
  6.5 56.1 %all-gather.4.cloned.1.call-start = ((), (), s32[]{:S(2)}) async-start(), calls=%async_computation | async-start | bytes 4456448 | tf_op jit(solution)/shard_map/all_gather | solution.py:107
  7.3 97.7 %all-gather.6.cloned.1.call-start = ((), (), s32[]{:S(2)}) async-start(), calls=%async_computation.1 | async-start | bytes 2228224 | tf_op jit(solution)/shard_map/all_gather | solution.py:114
  10.4 3.2 %copy-start.1 = (s32[8,12]{1,0:T(8,128)S(1)}, s32[8,12]{1,0:T(8,128)}, u32[]{:S(2)}) copy-start(s32[8,12]{1,0:T(8,128)} %param.14) | copy-start | bytes 1156
  62.7 3.4 %copy-start.4 = (bf16[4,2,512,512]{3,2,1,0:T(8,128)(2,1)S(1)}, bf16[4,2,512,512]{3,2,1,0:T(8,128)(2,1)}, u32[]{:S(2)}) copy-start(bf16[4,2,512,512]{3,2,1,0:T(8,128)(2,1)} %all-gather.4.cloned.1.call-done) | copy-start | bytes 12582916
Sparse Core Ops, SparseCore 0:
  9.5 53.1 all-gather.3
  64.8 40.0 all-gather.5

commit v2 on v1

--- a/solution.py
+++ b/solution.py
@@ -1,6 +1,8 @@
 import jax
 import jax.numpy as jnp
 from jax import lax
+from jax.experimental import pallas as pl
+from jax.experimental.pallas import tpu as pltpu
 from jax.sharding import PartitionSpec as P
 
 HIGHEST_PRECISION = lax.Precision.HIGHEST
@@ -147,12 +149,314 @@
     return jnp.concatenate([out_real, out_imag], axis=-1)
 
 
+BF = jnp.bfloat16
+F32 = jnp.float32
+
+
+def flip(value, pattern):
+    bit = 1
+    while bit <= pattern:
+        if pattern & bit:
+            value = value + bit - 2 * bit * ((value // bit) % 2)
+        bit *= 2
+    return value
+
+
+def iota(shape, axis):
+    return lax.broadcasted_iota(jnp.int32, shape, axis)
+
+
+def chain_kernel(
+    sizes, q_ref, f_ref, s_ref, cap_ref, out_ref,
+    qall, fall, mall, sel, tab, pick, name, gall, acc, pair_out, pair_in, ret_out, ret_in,
+    q_send, q_recv, f_send, f_recv, m_send, m_recv, p_send, p_recv, r_send, r_recv,
+):
+    chips, first_count, held, rows_piece, pieces, depth, half, wide = sizes
+    rows = pieces * rows_piece
+    held_rows = held * rows_piece
+    base = first_count * held
+    batch = chips // 2
+    me = lax.axis_index("bits")
+    core = me % 2
+    chip = me // 2
+    other = 1 - core
+    mate = 2 * chip + other
+
+    def near(pattern):
+        return flip(chip, pattern)
+
+    def send(src, dst, send_sem, recv_sem, device):
+        return pltpu.make_async_remote_copy(
+            src_ref=src, dst_ref=dst, send_sem=send_sem, recv_sem=recv_sem,
+            device_id={"bits": device}, device_id_type=pl.DeviceIdType.MESH,
+        )
+
+    barrier = pltpu.get_barrier_semaphore()
+    pl.semaphore_signal(
+        barrier, inc=1, device_id={"bits": mate}, device_id_type=pl.DeviceIdType.MESH
+    )
+    for t in range(1, chips):
+        pl.semaphore_signal(
+            barrier, inc=1, device_id={"bits": 2 * near(t) + core},
+            device_id_type=pl.DeviceIdType.MESH,
+        )
+
+    lane = iota((1, wide), 1)
+    sign = jnp.where(lane < wide // 2, -1.0, 1.0).astype(F32)
+
+    def turn(x):
+        return pltpu.roll(x, wide // 2, x.ndim - 1) * sign
+
+    closed = jnp.dot(s_ref[0], cap_ref[0], preferred_element_type=F32) + jnp.dot(
+        s_ref[1], cap_ref[1], preferred_element_type=F32
+    )
+    mall[chip] = closed.astype(BF)
+    fall[core] = f_ref[...]
+    qall[me] = q_ref[chip]
+
+    for a in range(first_count):
+        gap = iota((wide, held_rows), 1) - rows_piece * (iota((wide, held_rows), 0) - a * held)
+        inside = (gap >= 0) & (gap < rows_piece)
+        own = iota((wide, held_rows), 0) < (a + 1) * held
+        own = own & (iota((wide, held_rows), 0) >= a * held)
+        pick[a] = jnp.where(inside & own, 1.0, 0.0).astype(BF)
+    for b in range(2):
+        for q in range(batch):
+            row = base + 2 * near(2 * q + b) + core
+            hit = iota((wide, wide), 0) == row
+            name[b, :, q * wide:(q + 1) * wide] = jnp.where(hit, 1.0, 0.0).astype(BF)
+
+    pl.semaphore_wait(barrier, chips)
+
+    def q_direct(t):
+        target = near(t)
+        return send(q_ref.at[target], qall.at[me], q_send.at[t], q_recv.at[me], 2 * target + core)
+
+    def q_mate():
+        return send(q_ref.at[chip], qall.at[me], q_send.at[0], q_recv.at[me], mate)
+
+    def q_pass(t):
+        slot = 2 * near(t) + core
+        return send(qall.at[slot], qall.at[slot], q_send.at[chips + t], q_recv.at[slot], mate)
+
+    def f_copy(slot):
+        return send(f_ref, fall.at[slot], f_send, f_recv, mate)
+
+    def m_copy(slot, index, target):
+        return send(
+            mall.at[slot], mall.at[slot], m_send.at[index], m_recv.at[slot], 2 * target + core
+        )
+
+    lines = [2 * q for q in range(1, batch)]
+    for t in range(1, chips):
+        q_direct(t).start()
+    q_mate().start()
+    m_copy(chip, 1, near(1)).start()
+    for t in lines:
+        m_copy(chip, t, near(t)).start()
+    f_copy(core).start()
+
+    def m_arrived(slot):
+        m_copy(slot, 0, near(1)).wait_recv()
+
+    def q_arrived(slot):
+        send(q_ref.at[chip], qall.at[slot], q_send.at[0], q_recv.at[slot], mate).wait_recv()
+
+    same = (iota((rows, held_rows), 0) - iota((rows, held_rows), 1)) & (rows_piece - 1)
+    same = jnp.where(same == 0, 1.0, 0.0).astype(F32)
+
+    def prepare(slot):
+        block = qall[slot]
+        table = block[held_rows:].astype(F32)[:pieces]
+        spread = jnp.broadcast_to(table[:, None, :], (pieces, rows_piece, wide))
+        spread = spread.reshape(rows, wide).astype(BF)
+        tab[slot] = spread
+        for a in range(first_count):
+            chosen = jnp.dot(spread, pick[a], preferred_element_type=F32) * same
+            sel[slot, :, a * wide:(a + 1) * wide] = jnp.dot(
+                chosen.astype(BF), block[:held_rows], preferred_element_type=F32
+            ).astype(BF)
+
+    def gather_step(slot, b, q):
+        product = jnp.dot(
+            fall[...].reshape(4 * first_count * depth, half), mall[slot],
+            preferred_element_type=F32,
+        ).reshape(2, first_count, 2, depth, wide)
+        for c in range(2):
+            for a in range(first_count):
+                by_real, by_imag = product[c, a, 0], product[c, a, 1]
+                at = a * 4 * depth + c * depth
+                cols = slice(q * wide, (q + 1) * wide)
+                gall[b, at:at + depth, cols] = (by_real + turn(by_imag)).astype(BF)
+                gall[b, at + 2 * depth:at + 3 * depth, cols] = (turn(by_real) - by_imag).astype(BF)
+
+    for t in range(1, chips):
+        q_arrived(2 * near(t) + core)
+        q_pass(t).start()
+    f_copy(other).wait_recv()
+    gather_step(chip, 0, 0)
+
+    def prepare_own(c, carry):
+        prepare(2 * c + core)
+        return carry
+
+    def prepare_other(c, carry):
+        q_arrived(2 * c + other)
+        prepare(2 * c + other)
+        return carry
+
+    lax.fori_loop(0, chips, prepare_own, 0)
+    for t in lines:
+        m_arrived(near(t))
+        m_copy(near(t), t + 1, near(1)).start()
+        gather_step(near(t), 0, t // 2)
+    lax.fori_loop(0, chips, prepare_other, 0)
+
+    def part(slot, b):
+        values = jnp.dot(sel[slot], gall[b], preferred_element_type=F32)
+        named = jnp.dot(tab[slot], name[b], preferred_element_type=F32)
+        values = values * named
+        total = values[:, :wide]
+        for q in range(1, batch):
+            total = total + values[:, q * wide:(q + 1) * wide]
+        return total
+
+    def first_half(slot, carry):
+        acc[slot] = part(slot, 0)
+        return carry
+
+    lax.fori_loop(0, 2 * chips, first_half, 0)
+    for q in range(batch):
+        m_arrived(near(2 * q + 1))
+        gather_step(near(2 * q + 1), 1, q)
+
+    def pair_copy(c):
+        return send(pair_out.at[c], pair_in.at[c], p_send.at[c], p_recv.at[c], mate)
+
+    def second_other(c, carry):
+        slot = 2 * c + other
+        pair_out[c] = (acc[slot] + part(slot, 1)).astype(BF)
+        pair_copy(c).start()
+        return carry
+
+    def second_own(c, carry):
+        slot = 2 * c + core
+        acc[slot] = acc[slot] + part(slot, 1)
+        return carry
+
+    lax.fori_loop(0, chips, second_other, 0)
+    lax.fori_loop(0, chips, second_own, 0)
+
+    def ret_copy(t):
+        target = near(t)
+        return send(
+            ret_out.at[target], ret_in.at[chip], r_send.at[t], r_recv.at[chip], 2 * target + core
+        )
+
+    def ret_arrived(source):
+        send(
+            ret_out.at[source], ret_in.at[source], r_send.at[0], r_recv.at[source],
+            2 * source + core,
+        ).wait_recv()
+
+    for t in range(chips - 1, 0, -1):
+        target = near(t)
+        pair_copy(target).wait_recv()
+        ret_out[target] = (acc[2 * target + core] + pair_in[target].astype(F32)).astype(BF)
+        ret_copy(t).start()
+    pair_copy(chip).wait_recv()
+    total = acc[me] + pair_in[chip].astype(F32)
+    for t in range(1, chips):
+        ret_arrived(near(t))
+        total = total + ret_in[near(t)].astype(F32)
+    out_ref[...] = total
+
+    q_mate().wait_send()
+    f_copy(core).wait_send()
+    m_copy(chip, 1, near(1)).wait_send()
+    for t in lines:
+        m_copy(chip, t, near(t)).wait_send()
+        m_copy(near(t), t + 1, near(1)).wait_send()
+    for t in range(1, chips):
+        q_direct(t).wait_send()
+        q_pass(t).wait_send()
+        ret_copy(t).wait_send()
+    for c in range(chips):
+        pair_copy(c).wait_send()
+
+
+def on_device_chain(prefix, first_suffix, pair_prefix, pair_suffix, merge_count, suffix, routes, cap):
+    pieces = pair_prefix.shape[0]
+    held, rows_piece, twice_width = prefix.shape
+    half = twice_width // 2
+    first_count, _, depth, _ = first_suffix.shape
+    owners = lax.axis_size("bits")
+    listed = routes.shape[1]
+    chips = owners // 2
+    wide = 2 * cap.shape[2]
+    rows = pieces * rows_piece
+    held_rows = held * rows_piece
+    picks = weights_of(pair_prefix, pair_suffix, merge_count, held, first_count)
+    named = jnp.sum(
+        (routes[:, :, None] == lax.broadcasted_iota(jnp.int32, (pieces, listed, owners), 2)).astype(F32),
+        axis=1,
+    ).astype(BF)
+    table = jnp.concatenate([picks.reshape(pieces, first_count * held), named], axis=1)
+    table = jnp.pad(table, ((0, 16 - pieces), (0, wide - table.shape[1])))
+    columns = prefix.reshape(held_rows, 2, chips, 2 * depth).transpose(2, 0, 1, 3)
+    columns = columns.reshape(chips, held_rows, wide)
+    packed = jnp.concatenate(
+        [columns, jnp.broadcast_to(table[None], (chips, 16, wide))], axis=1
+    )
+    caps = jnp.stack(
+        [jnp.concatenate([cap[0], cap[1]], axis=1), jnp.concatenate([-cap[1], cap[0]], axis=1)]
+    )
+    sizes = (chips, first_count, held, rows_piece, pieces, depth, half, wide)
+    batch = chips // 2
+    vmem = pl.BlockSpec(memory_space=pltpu.VMEM)
+    dma = pltpu.SemaphoreType.DMA
+    sent = pltpu.VMEM((chips, rows, wide), BF)
+    out = pl.pallas_call(
+        lambda *refs: chain_kernel(sizes, *refs),
+        name="chain",
+        out_shape=jax.ShapeDtypeStruct((rows, wide), F32),
+        in_specs=[vmem] * 4,
+        out_specs=vmem,
+        scratch_shapes=[
+            pltpu.VMEM((owners, held_rows + 16, wide), BF),
+            pltpu.VMEM((2, first_count, 2, depth, half), BF),
+            pltpu.VMEM((chips, half, wide), BF),
+            pltpu.VMEM((owners, rows, first_count * wide), BF),
+            pltpu.VMEM((owners, rows, wide), BF),
+            pltpu.VMEM((first_count, wide, held_rows), BF),
+            pltpu.VMEM((2, wide, batch * wide), BF),
+            pltpu.VMEM((2, first_count * wide, batch * wide), BF),
+            pltpu.VMEM((owners, rows, wide), F32),
+            sent, sent, sent, sent,
+            dma((2 * chips,)), dma((owners,)), dma, dma, dma((chips,)), dma((chips,)),
+            dma((chips,)), dma((chips,)), dma((chips,)), dma((chips,)),
+        ],
+        compiler_params=pltpu.CompilerParams(collective_id=0, has_side_effects=True),
+    )(packed, first_suffix, suffix[0], caps)
+    return out.reshape(pieces, rows_piece, wide)
+
+
 def on_device(prefix, first_suffix, pair_prefix, pair_suffix, merge_count, suffix, routes, cap):
     pieces = pair_prefix.shape[0]
     listed = routes.shape[1]
     owners = lax.axis_size("bits")
     slots = min(pieces, max(2, (2 * pieces * listed + owners - 1) // owners))
-    body = on_device_dense if slots == pieces else on_device_sparse
+    chips = owners // 2
+    held, rows_piece, twice_width = prefix.shape
+    wide = 2 * cap.shape[2]
+    fits = (
+        owners % 4 == 0 and chips & (chips - 1) == 0 and wide == 128 and pieces == 8
+        and twice_width == chips * wide and first_suffix.shape[0] * held + owners <= wide
+        and suffix.shape[0] == 1 and rows_piece == 16 and first_suffix.shape[2] % 16 == 0
+    )
+    body = on_device_sparse
+    if slots == pieces:
+        body = on_device_chain if fits else on_device_dense
     return body(
         prefix, first_suffix, pair_prefix, pair_suffix, merge_count, suffix, routes, cap
     )

time: 116 us -> 52.5 us (0.45)
  waiting for transfers between devices: 87.5 us -> 0 us
  Pallas kernels: 0 us -> 44.9 us
  between operations: 13.6 us -> 0.09 us
  matrix products: 10.5 us -> 0 us
  local copies, waits for them, and re-layouts: 1.96 us -> 4.78 us
    all_gather x2 -> x0, waiting for transfers between devices: 86.8 us -> none  [the longest x1 48.8 us: on_device_dense(): portion = lax.all_gather(first_suffix, 'bits', axis=2, tiled=True)]
    pallas_call x0 -> x1, Pallas kernels: none -> 44.9 us  [on_device_chain(): pl.pallas_call(lambda *refs: chain_kernel(sizes, *refs), name='chain', ou...]
    dot_general x6 -> x0, matrix products: 10.5 us -> none  [the longest x1 3.04 us: on_device_dense(): jnp.einsum('arc,acw->rw', jnp.concatenate([real, -imag], axis=2), portion...]
    unnamed x13 -> x12, local copies, waits for them, and re-layouts: 0.5 us -> 3.29 us
  transfers between devices with their start and end apart: 2 -> 0, of which waited for: 2 -> 0; matrix products, arithmetic and copies ran while one was open for 9% -> 0% of each run, Pallas kernels for 0% -> 0%
where the time goes in v2:
time: 52.5 us; the launch traced here: 52.2 us
  Pallas kernels  44.9 us (86%)
  local copies, waits for them, and re-layouts  4.78 us (9%)
  other arithmetic  2.45 us (5%)
    pallas_call x1, Pallas kernels, on_device_chain(): pl.pallas_call(lambda *refs: chain_kernel(sizes, *refs), name='chain', ou...  44.9 us
    unnamed x12, local copies, waits for them, and re-layouts  3.29 us

profile of v2, /device:TPU:0, one launch (start us, length us, event | category | flops | bytes accessed | tf_op | source)
XLA Modules:
  0.0 52.2 jit_solution(4306575896676414179)
XLA Ops:
  0.0 0.0 copy-start.3
  0.0 0.0 copy-start.2
  0.0 0.7 %copy-done.3 = s32[8]{0:T(128)S(1)} copy-done((s32[8]{0:T(128)S(1)}, s32[8]{0:T(128)}, u32[]{:S(2)}) %copy-start.3) | copy-done | bytes 56
  0.7 0.0 copy-done.2
  0.7 0.7 %iota_compare_fusion.3 = (pred[8,3,4]{0,2,1:T(4,128)(4,1)S(1)}, pred[8,3,4]{0,2,1:T(4,128)(4,1)S(1)}) fusion(s32[8,3]{0,1:T(4,128)S(1)} %copy-done.2, pred[8,3]{0,1:T(4,128)(4,1)S(1)} %iota_compare_fusion.5, s32[8,3]{0,1:T(4,128)} %param.11), kind=kLoop, calls=%fused_computation.15 | loop fusion | flops 288 | bytes 408 | tf_op jit(solution)/shard_map/eq | solution.py:95
  1.4 0.0 copy-start.1
  1.4 0.1 copy.23
  1.5 0.6 %copy-done.1 = s32[8,12]{1,0:T(8,128)S(1)} copy-done((s32[8,12]{1,0:T(8,128)S(1)}, s32[8,12]{1,0:T(8,128)}, u32[]{:S(2)}) %copy-start.1) | copy-done | bytes 408
  2.1 0.1 copy.22
  2.2 0.1 convert_reduce_fusion
  2.3 0.1 fusion.6
  2.4 0.9 %fusion.7 = (bf16[1,512,64]{1,2,0:T(8,128)(2,1)S(1)}, bf16[1,512,64]{1,2,0:T(8,128)(2,1)S(1)}) fusion(bf16[2,512,64]{1,2,0:T(8,128)(2,1)} %param.15), kind=kLoop, calls=%fused_computation.21 | loop fusion | bytes 262144 | tf_op jit(solution)/shard_map/slice | solution.py:412
  3.2 0.1 copy.27
  3.4 0.1 copy.26
  3.5 0.1 maximum_bitcast_fusion
  3.7 0.0 copy-start
  3.7 0.7 %pad_maximum_fusion.refs_3_ = bf16[2,512,128]{2,1,0:T(8,128)(2,1)} fusion(bf16[1,512,128]{2,1,0:T(8,128)(2,1)S(1)} %get-tuple-element.6, bf16[1,512,128]{2,1,0:T(8,128)(2,1)S(1)} %get-tuple-element.5), kind=kLoop, calls=%fused_computation | loop fusion | flops 131072 | bytes 524288 | tf_op jit(solution)/shard_map/stack | solution.py:411
  4.4 0.2 copy-done
  4.6 0.2 reshape.44
  4.8 0.2 copy.29
  5.0 0.1 reshape.45
  5.2 0.7 %pad_maximum_fusion.1.refs_0_ = bf16[8,80,128]{2,1,0:T(8,128)(2,1)} fusion(bf16[8,16,128]{2,1,0:T(8,128)(2,1)S(1)} %broadcast_in_dim.2, bf16[8,64,128]{2,1,0:T(8,128)(2,1)S(1)} %reshape.45), kind=kLoop, calls=%fused_computation.2 | loop fusion | flops 327680 | bytes 327680 | tf_op jit(solution)/shard_map/concatenate | solution.py:408
  5.8 44.9 %chain.1 = f32[128,128]{1,0:T(8,128)} custom-call(bf16[8,80,128]{2,1,0:T(8,128)(2,1)} %pad_maximum_fusion.1.refs_0_, bf16[4,2,32,512]{3,2,1,0:T(8,128)(2,1)} %refs_1_.1, bf16[2,512,512]{2,1,0:T(8,128)(2,1)} %bitcast.14, bf16[2,512,128]{2,1,0:T(8,128)(2,1)} %pad_maximum_fusion.refs_3_), custom_call_target="tpu_custom_call" | custom-call | tf_op jit(solution)/shard_map/chain/pallas_call | solution.py:419
  50.7 1.5 %copy.31 = f32[8,16,128]{2,1,0:T(8,128)} copy(f32[8,16,128]{2,1,0:T(8,128)} %bitcast.17) | data formatting | bytes 131072
  (4 shorter events, 0.1 us)
Async XLA Ops:
  0.0 0.7 %copy-start.3 = (s32[8]{0:T(128)S(1)}, s32[8]{0:T(128)}, u32[]{:S(2)}) copy-start(s32[8]{0:T(128)} %param.12) | copy-start | bytes 100
  0.0 0.7 %copy-start.2 = (s32[8,3]{0,1:T(4,128)S(1)}, s32[8,3]{0,1:T(4,128)}, u32[]{:S(2)}) copy-start(s32[8,3]{0,1:T(4,128)} %param.10) | copy-start | bytes 292
  1.4 0.7 %copy-start.1 = (s32[8,12]{1,0:T(8,128)S(1)}, s32[8,12]{1,0:T(8,128)}, u32[]{:S(2)}) copy-start(s32[8,12]{1,0:T(8,128)} %param.14) | copy-start | bytes 1156
  3.7 0.9 %copy-start = (bf16[4,16,1024]{2,1,0:T(8,128)(2,1)S(1)}, bf16[4,16,1024]{2,1,0:T(8,128)(2,1)}, u32[]{:S(2)}) copy-start(bf16[4,16,1024]{2,1,0:T(8,128)(2,1)} %param.8) | copy-start | bytes 393220

commit v3 on v2

--- a/solution.py
+++ b/solution.py
@@ -176,6 +176,7 @@
     held_rows = held * rows_piece
     base = first_count * held
     batch = chips // 2
+    bundle = min(4, chips)
     me = lax.axis_index("bits")
     core = me % 2
     chip = me // 2
@@ -212,14 +213,13 @@
     )
     mall[chip] = closed.astype(BF)
     fall[core] = f_ref[...]
-    qall[me] = q_ref[chip]
+    qall[0, chip] = q_ref[chip]
 
     for a in range(first_count):
-        gap = iota((wide, held_rows), 1) - rows_piece * (iota((wide, held_rows), 0) - a * held)
-        inside = (gap >= 0) & (gap < rows_piece)
-        own = iota((wide, held_rows), 0) < (a + 1) * held
-        own = own & (iota((wide, held_rows), 0) >= a * held)
-        pick[a] = jnp.where(inside & own, 1.0, 0.0).astype(BF)
+        line = iota((wide, wide), 0) - a * held
+        gap = iota((wide, wide), 1) - rows_piece * line
+        inside = (gap >= 0) & (gap < rows_piece) & (line >= 0) & (line < held)
+        pick[:, a * wide:(a + 1) * wide] = jnp.where(inside, 1.0, 0.0).astype(BF)
     for b in range(2):
         for q in range(batch):
             row = base + 2 * near(2 * q + b) + core
@@ -230,14 +230,19 @@
 
     def q_direct(t):
         target = near(t)
-        return send(q_ref.at[target], qall.at[me], q_send.at[t], q_recv.at[me], 2 * target + core)
+        return send(
+            q_ref.at[target], qall.at[0, chip], q_send.at[t], q_recv.at[0, chip],
+            2 * target + core,
+        )
 
     def q_mate():
-        return send(q_ref.at[chip], qall.at[me], q_send.at[0], q_recv.at[me], mate)
+        return send(q_ref.at[chip], qall.at[1, chip], q_send.at[0], q_recv.at[1, chip], mate)
 
     def q_pass(t):
-        slot = 2 * near(t) + core
-        return send(qall.at[slot], qall.at[slot], q_send.at[chips + t], q_recv.at[slot], mate)
+        slot = near(t)
+        return send(
+            qall.at[0, slot], qall.at[1, slot], q_send.at[chips + t], q_recv.at[1, slot], mate
+        )
 
     def f_copy(slot):
         return send(f_ref, fall.at[slot], f_send, f_recv, mate)
@@ -259,23 +264,32 @@
     def m_arrived(slot):
         m_copy(slot, 0, near(1)).wait_recv()
 
-    def q_arrived(slot):
-        send(q_ref.at[chip], qall.at[slot], q_send.at[0], q_recv.at[slot], mate).wait_recv()
-
-    same = (iota((rows, held_rows), 0) - iota((rows, held_rows), 1)) & (rows_piece - 1)
+    def q_arrived(kind, slot):
+        send(
+            q_ref.at[chip], qall.at[kind, slot], q_send.at[0], q_recv.at[kind, slot], mate
+        ).wait_recv()
+
+    full = first_count * wide
+    same = (iota((rows, full), 0) - iota((rows, full), 1)) & (rows_piece - 1)
     same = jnp.where(same == 0, 1.0, 0.0).astype(F32)
 
-    def prepare(slot):
-        block = qall[slot]
-        table = block[held_rows:].astype(F32)[:pieces]
-        spread = jnp.broadcast_to(table[:, None, :], (pieces, rows_piece, wide))
-        spread = spread.reshape(rows, wide).astype(BF)
-        tab[slot] = spread
-        for a in range(first_count):
-            chosen = jnp.dot(spread, pick[a], preferred_element_type=F32) * same
-            sel[slot, :, a * wide:(a + 1) * wide] = jnp.dot(
-                chosen.astype(BF), block[:held_rows], preferred_element_type=F32
-            ).astype(BF)
+    def prepare(kind, group):
+        first = group * bundle
+        blocks = [qall[kind, first + u] for u in range(bundle)]
+        for u, block in enumerate(blocks):
+            table = block[held_rows:].astype(F32)[:pieces]
+            spread = jnp.broadcast_to(table[:, None, :], (pieces, rows_piece, wide))
+            tab[kind, first + u] = spread.reshape(rows, wide).astype(BF)
+        spreads = tab[kind, pl.ds(first, bundle)].reshape(bundle * rows, wide)
+        chosen = jnp.dot(spreads, pick[...], preferred_element_type=F32)
+        for u, block in enumerate(blocks):
+            kept = (chosen[u * rows:(u + 1) * rows] * same).astype(BF)
+            stacked = jnp.concatenate(
+                [kept[:, a * wide:a * wide + held_rows] for a in range(first_count)], axis=0
+            )
+            picked = jnp.dot(stacked, block[:held_rows], preferred_element_type=F32).astype(BF)
+            for a in range(first_count):
+                sel[kind, first + u, :, a * wide:(a + 1) * wide] = picked[a * rows:(a + 1) * rows]
 
     def gather_step(slot, b, q):
         product = jnp.dot(
@@ -291,41 +305,47 @@
                 gall[b, at + 2 * depth:at + 3 * depth, cols] = (turn(by_real) - by_imag).astype(BF)
 
     for t in range(1, chips):
-        q_arrived(2 * near(t) + core)
+        q_arrived(0, near(t))
         q_pass(t).start()
     f_copy(other).wait_recv()
     gather_step(chip, 0, 0)
 
-    def prepare_own(c, carry):
-        prepare(2 * c + core)
+    def prepare_own(group, carry):
+        prepare(0, group)
         return carry
 
-    def prepare_other(c, carry):
-        q_arrived(2 * c + other)
-        prepare(2 * c + other)
+    def prepare_other(group, carry):
+        for u in range(bundle):
+            q_arrived(1, group * bundle + u)
+        prepare(1, group)
         return carry
 
-    lax.fori_loop(0, chips, prepare_own, 0)
+    groups = chips // bundle
+    lax.fori_loop(0, groups, prepare_own, 0)
     for t in lines:
         m_arrived(near(t))
         m_copy(near(t), t + 1, near(1)).start()
         gather_step(near(t), 0, t // 2)
-    lax.fori_loop(0, chips, prepare_other, 0)
-
-    def part(slot, b):
-        values = jnp.dot(sel[slot], gall[b], preferred_element_type=F32)
-        named = jnp.dot(tab[slot], name[b], preferred_element_type=F32)
+    lax.fori_loop(0, groups, prepare_other, 0)
+
+    def part(kind, group, b):
+        first = pl.ds(group * bundle, bundle)
+        lines_sel = sel[kind, first].reshape(bundle * rows, full)
+        lines_tab = tab[kind, first].reshape(bundle * rows, wide)
+        values = jnp.dot(lines_sel, gall[b], preferred_element_type=F32)
+        named = jnp.dot(lines_tab, name[b], preferred_element_type=F32)
         values = values * named
         total = values[:, :wide]
         for q in range(1, batch):
             total = total + values[:, q * wide:(q + 1) * wide]
-        return total
-
-    def first_half(slot, carry):
-        acc[slot] = part(slot, 0)
-        return carry
-
-    lax.fori_loop(0, 2 * chips, first_half, 0)
+        return total.reshape(bundle, rows, wide)
+
+    for kind in (1, 0):
+        def first_half(group, carry):
+            acc[kind, pl.ds(group * bundle, bundle)] = part(kind, group, 0)
+            return carry
+
+        lax.fori_loop(0, groups, first_half, 0)
     for q in range(batch):
         m_arrived(near(2 * q + 1))
         gather_step(near(2 * q + 1), 1, q)
@@ -333,19 +353,20 @@
     def pair_copy(c):
         return send(pair_out.at[c], pair_in.at[c], p_send.at[c], p_recv.at[c], mate)
 
-    def second_other(c, carry):
-        slot = 2 * c + other
-        pair_out[c] = (acc[slot] + part(slot, 1)).astype(BF)
-        pair_copy(c).start()
+    def second_other(group, carry):
+        first = pl.ds(group * bundle, bundle)
+        pair_out[first] = (acc[1, first] + part(1, group, 1)).astype(BF)
+        for u in range(bundle):
+            pair_copy(group * bundle + u).start()
         return carry
 
-    def second_own(c, carry):
-        slot = 2 * c + core
-        acc[slot] = acc[slot] + part(slot, 1)
+    def second_own(group, carry):
+        first = pl.ds(group * bundle, bundle)
+        acc[0, first] = acc[0, first] + part(0, group, 1)
         return carry
 
-    lax.fori_loop(0, chips, second_other, 0)
-    lax.fori_loop(0, chips, second_own, 0)
+    lax.fori_loop(0, groups, second_other, 0)
+    lax.fori_loop(0, groups, second_own, 0)
 
     def ret_copy(t):
         target = near(t)
@@ -362,10 +383,10 @@
     for t in range(chips - 1, 0, -1):
         target = near(t)
         pair_copy(target).wait_recv()
-        ret_out[target] = (acc[2 * target + core] + pair_in[target].astype(F32)).astype(BF)
+        ret_out[target] = (acc[0, target] + pair_in[target].astype(F32)).astype(BF)
         ret_copy(t).start()
     pair_copy(chip).wait_recv()
-    total = acc[me] + pair_in[chip].astype(F32)
+    total = acc[0, chip] + pair_in[chip].astype(F32)
     for t in range(1, chips):
         ret_arrived(near(t))
         total = total + ret_in[near(t)].astype(F32)
@@ -423,17 +444,17 @@
         in_specs=[vmem] * 4,
         out_specs=vmem,
         scratch_shapes=[
-            pltpu.VMEM((owners, held_rows + 16, wide), BF),
+            pltpu.VMEM((2, chips, held_rows + 16, wide), BF),
             pltpu.VMEM((2, first_count, 2, depth, half), BF),
             pltpu.VMEM((chips, half, wide), BF),
-            pltpu.VMEM((owners, rows, first_count * wide), BF),
-            pltpu.VMEM((owners, rows, wide), BF),
-            pltpu.VMEM((first_count, wide, held_rows), BF),
+            pltpu.VMEM((2, chips, rows, first_count * wide), BF),
+            pltpu.VMEM((2, chips, rows, wide), BF),
+            pltpu.VMEM((wide, first_count * wide), BF),
             pltpu.VMEM((2, wide, batch * wide), BF),
             pltpu.VMEM((2, first_count * wide, batch * wide), BF),
-            pltpu.VMEM((owners, rows, wide), F32),
+            pltpu.VMEM((2, chips, rows, wide), F32),
             sent, sent, sent, sent,
-            dma((2 * chips,)), dma((owners,)), dma, dma, dma((chips,)), dma((chips,)),
+            dma((2 * chips,)), dma((2, chips)), dma, dma, dma((chips,)), dma((chips,)),
             dma((chips,)), dma((chips,)), dma((chips,)), dma((chips,)),
         ],
         compiler_params=pltpu.CompilerParams(collective_id=0, has_side_effects=True),

time: 52.5 us -> 47.4 us (0.903)
  Pallas kernels: 44.9 us -> 39.8 us
    pallas_call x1, Pallas kernels: 44.9 us -> 39.8 us  [on_device_chain(): pl.pallas_call(lambda *refs: chain_kernel(sizes, *refs), name='chain', ou...]
where the time goes in v3:
time: 47.4 us; the launch traced here: 47.1 us
  Pallas kernels  39.8 us (84%)
  local copies, waits for them, and re-layouts  4.78 us (10%)
  other arithmetic  2.45 us (5%)
    pallas_call x1, Pallas kernels, on_device_chain(): pl.pallas_call(lambda *refs: chain_kernel(sizes, *refs), name='chain', ou...  39.8 us
    unnamed x12, local copies, waits for them, and re-layouts  3.29 us

profile of v3, /device:TPU:0, one launch (start us, length us, event | category | flops | bytes accessed | tf_op | source)
XLA Modules:
  0.0 47.1 jit_solution(10771170737137142873)
XLA Ops:
  0.0 0.0 copy-start.3
  0.0 0.0 copy-start.2
  0.0 0.7 %copy-done.3 = s32[8]{0:T(128)S(1)} copy-done((s32[8]{0:T(128)S(1)}, s32[8]{0:T(128)}, u32[]{:S(2)}) %copy-start.3) | copy-done | bytes 56
  0.7 0.0 copy-done.2
  0.7 0.7 %iota_compare_fusion.3 = (pred[8,3,4]{0,2,1:T(4,128)(4,1)S(1)}, pred[8,3,4]{0,2,1:T(4,128)(4,1)S(1)}) fusion(s32[8,3]{0,1:T(4,128)S(1)} %copy-done.2, pred[8,3]{0,1:T(4,128)(4,1)S(1)} %iota_compare_fusion.5, s32[8,3]{0,1:T(4,128)} %param.11), kind=kLoop, calls=%fused_computation.15 | loop fusion | flops 288 | bytes 408 | tf_op jit(solution)/shard_map/eq | solution.py:95
  1.4 0.0 copy-start.1
  1.4 0.1 copy.23
  1.5 0.6 %copy-done.1 = s32[8,12]{1,0:T(8,128)S(1)} copy-done((s32[8,12]{1,0:T(8,128)S(1)}, s32[8,12]{1,0:T(8,128)}, u32[]{:S(2)}) %copy-start.1) | copy-done | bytes 408
  2.1 0.1 copy.22
  2.2 0.1 convert_reduce_fusion
  2.3 0.1 fusion.6
  2.4 0.9 %fusion.7 = (bf16[1,512,64]{1,2,0:T(8,128)(2,1)S(1)}, bf16[1,512,64]{1,2,0:T(8,128)(2,1)S(1)}) fusion(bf16[2,512,64]{1,2,0:T(8,128)(2,1)} %param.15), kind=kLoop, calls=%fused_computation.21 | loop fusion | bytes 262144 | tf_op jit(solution)/shard_map/slice | solution.py:433
  3.2 0.1 copy.27
  3.4 0.1 copy.26
  3.5 0.1 maximum_bitcast_fusion
  3.7 0.0 copy-start
  3.7 0.7 %pad_maximum_fusion.refs_3_ = bf16[2,512,128]{2,1,0:T(8,128)(2,1)} fusion(bf16[1,512,128]{2,1,0:T(8,128)(2,1)S(1)} %get-tuple-element.6, bf16[1,512,128]{2,1,0:T(8,128)(2,1)S(1)} %get-tuple-element.5), kind=kLoop, calls=%fused_computation | loop fusion | flops 131072 | bytes 524288 | tf_op jit(solution)/shard_map/stack | solution.py:432
  4.4 0.2 copy-done
  4.6 0.2 reshape.44
  4.8 0.2 copy.29
  5.0 0.1 reshape.45
  5.2 0.7 %pad_maximum_fusion.1.refs_0_ = bf16[8,80,128]{2,1,0:T(8,128)(2,1)} fusion(bf16[8,16,128]{2,1,0:T(8,128)(2,1)S(1)} %broadcast_in_dim.2, bf16[8,64,128]{2,1,0:T(8,128)(2,1)S(1)} %reshape.45), kind=kLoop, calls=%fused_computation.2 | loop fusion | flops 327680 | bytes 327680 | tf_op jit(solution)/shard_map/concatenate | solution.py:429
  5.8 39.8 %chain.1 = f32[128,128]{1,0:T(8,128)} custom-call(bf16[8,80,128]{2,1,0:T(8,128)(2,1)} %pad_maximum_fusion.1.refs_0_, bf16[4,2,32,512]{3,2,1,0:T(8,128)(2,1)} %refs_1_.1, bf16[2,512,512]{2,1,0:T(8,128)(2,1)} %bitcast.14, bf16[2,512,128]{2,1,0:T(8,128)(2,1)} %pad_maximum_fusion.refs_3_), custom_call_target="tpu_custom_call" | custom-call | tf_op jit(solution)/shard_map/chain/pallas_call | solution.py:440
  45.6 1.5 %copy.31 = f32[8,16,128]{2,1,0:T(8,128)} copy(f32[8,16,128]{2,1,0:T(8,128)} %bitcast.17) | data formatting | bytes 131072
  (4 shorter events, 0.1 us)
Async XLA Ops:
  0.0 0.7 %copy-start.3 = (s32[8]{0:T(128)S(1)}, s32[8]{0:T(128)}, u32[]{:S(2)}) copy-start(s32[8]{0:T(128)} %param.12) | copy-start | bytes 100
  0.0 0.7 %copy-start.2 = (s32[8,3]{0,1:T(4,128)S(1)}, s32[8,3]{0,1:T(4,128)}, u32[]{:S(2)}) copy-start(s32[8,3]{0,1:T(4,128)} %param.10) | copy-start | bytes 292
  1.4 0.7 %copy-start.1 = (s32[8,12]{1,0:T(8,128)S(1)}, s32[8,12]{1,0:T(8,128)}, u32[]{:S(2)}) copy-start(s32[8,12]{1,0:T(8,128)} %param.14) | copy-start | bytes 1156
  3.7 0.9 %copy-start = (bf16[4,16,1024]{2,1,0:T(8,128)(2,1)S(1)}, bf16[4,16,1024]{2,1,0:T(8,128)(2,1)}, u32[]{:S(2)}) copy-start(bf16[4,16,1024]{2,1,0:T(8,128)(2,1)} %param.8) | copy-start | bytes 393220

commit v4 on v3

--- a/solution.py
+++ b/solution.py
@@ -167,8 +167,8 @@
 
 
 def chain_kernel(
-    sizes, q_ref, f_ref, s_ref, cap_ref, out_ref,
-    qall, fall, mall, sel, tab, pick, name, gall, acc, pair_out, pair_in, ret_out, ret_in,
+    sizes, x_ref, code_ref, count_ref, route_ref, f_ref, s_ref, cap_ref, out_ref,
+    q_ref, qall, fall, mall, sel, tab, pick, name, gall, acc, pair_out, pair_in, ret_out, ret_in,
     q_send, q_recv, f_send, f_recv, m_send, m_recv, p_send, p_recv, r_send, r_recv,
 ):
     chips, first_count, held, rows_piece, pieces, depth, half, wide = sizes
@@ -208,10 +208,28 @@
     def turn(x):
         return pltpu.roll(x, wide // 2, x.ndim - 1) * sign
 
-    closed = jnp.dot(s_ref[0], cap_ref[0], preferred_element_type=F32) + jnp.dot(
-        s_ref[1], cap_ref[1], preferred_element_type=F32
-    )
-    mall[chip] = closed.astype(BF)
+    spot = iota((pieces, wide), 1)
+    table = jnp.zeros((pieces, wide), F32)
+    for k in range(code_ref.shape[1]):
+        hit = (spot == code_ref[:, k:k + 1]) & (count_ref[...] > k)
+        table = table + jnp.where(hit, 1.0, 0.0)
+    for k in range(route_ref.shape[1]):
+        table = table + jnp.where(spot == route_ref[:, k:k + 1] + base, 1.0, 0.0)
+    table = jnp.concatenate([table, jnp.zeros((16 - pieces, wide), F32)], axis=0)
+    x = x_ref[...].astype(F32)
+    for c in range(chips):
+        at = c * (wide // 2)
+        q_ref[c, :held_rows] = jnp.concatenate(
+            [x[:, at:at + wide // 2], x[:, half + at:half + at + wide // 2]], axis=1
+        ).astype(BF)
+        q_ref[c, held_rows:] = table.astype(BF)
+
+    def times_cap(block):
+        return lax.dot_general(
+            block, cap_ref[...], (((1,), (1,)), ((), ())), preferred_element_type=F32
+        )
+
+    mall[chip] = (times_cap(s_ref[0]) + turn(times_cap(s_ref[1]))).astype(BF)
     fall[core] = f_ref[...]
     qall[0, chip] = q_ref[chip]
 
@@ -412,26 +430,13 @@
     half = twice_width // 2
     first_count, _, depth, _ = first_suffix.shape
     owners = lax.axis_size("bits")
-    listed = routes.shape[1]
     chips = owners // 2
     wide = 2 * cap.shape[2]
     rows = pieces * rows_piece
     held_rows = held * rows_piece
-    picks = weights_of(pair_prefix, pair_suffix, merge_count, held, first_count)
-    named = jnp.sum(
-        (routes[:, :, None] == lax.broadcasted_iota(jnp.int32, (pieces, listed, owners), 2)).astype(F32),
-        axis=1,
-    ).astype(BF)
-    table = jnp.concatenate([picks.reshape(pieces, first_count * held), named], axis=1)
-    table = jnp.pad(table, ((0, 16 - pieces), (0, wide - table.shape[1])))
-    columns = prefix.reshape(held_rows, 2, chips, 2 * depth).transpose(2, 0, 1, 3)
-    columns = columns.reshape(chips, held_rows, wide)
-    packed = jnp.concatenate(
-        [columns, jnp.broadcast_to(table[None], (chips, 16, wide))], axis=1
-    )
-    caps = jnp.stack(
-        [jnp.concatenate([cap[0], cap[1]], axis=1), jnp.concatenate([-cap[1], cap[0]], axis=1)]
-    )
+    code = pair_suffix * held + pair_prefix
+    count = merge_count[:, None]
+    caps = cap.transpose(0, 2, 1).reshape(wide, half)
     sizes = (chips, first_count, held, rows_piece, pieces, depth, half, wide)
     batch = chips // 2
     vmem = pl.BlockSpec(memory_space=pltpu.VMEM)
@@ -441,9 +446,10 @@
         lambda *refs: chain_kernel(sizes, *refs),
         name="chain",
         out_shape=jax.ShapeDtypeStruct((rows, wide), F32),
-        in_specs=[vmem] * 4,
+        in_specs=[vmem] * 7,
         out_specs=vmem,
         scratch_shapes=[
+            pltpu.VMEM((chips, held_rows + 16, wide), BF),
             pltpu.VMEM((2, chips, held_rows + 16, wide), BF),
             pltpu.VMEM((2, first_count, 2, depth, half), BF),
             pltpu.VMEM((chips, half, wide), BF),
@@ -458,7 +464,7 @@
             dma((chips,)), dma((chips,)), dma((chips,)), dma((chips,)),
         ],
         compiler_params=pltpu.CompilerParams(collective_id=0, has_side_effects=True),
-    )(packed, first_suffix, suffix[0], caps)
+    )(prefix.reshape(held_rows, twice_width), code, count, routes, first_suffix, suffix[0], caps)
     return out.reshape(pieces, rows_piece, wide)
 
 

time: 47.4 us -> 44.2 us (0.932)
  other arithmetic: 2.45 us -> 0.6 us
  local copies, waits for them, and re-layouts: 4.78 us -> 3.65 us
    slice x1 -> x0, local copies, waits for them, and re-layouts: 0.88 us -> none  [on_device_chain(): cap[1]]
    another operation x2 -> x0, other arithmetic: 0.86 us -> none  [on_device_chain(): jnp.stack([jnp.concatenate([cap[0], cap[1]], axis=1), jnp.concatenate([-c...]
    concatenate x2 -> x0, other arithmetic: 0.76 us -> none  [the longest x1 0.68 us: on_device_chain(): jnp.concatenate([columns, jnp.broadcast_to(table[None], (chips, 16, wide)...]
    eq x1 -> x0, other arithmetic: 0.69 us -> none  [weights_of(): pair_prefix[:, :, None]]
    broadcast_in_dim x1, local copies, waits for them, and re-layouts: 0.01 us -> 0.67 us  [on_device_chain(): count = merge_count[:, None]]
    add x0 -> x1, other arithmetic: none -> 0.6 us  [on_device_chain(): code = pair_suffix * held + pair_prefix]
    reshape x3 -> x0, local copies, waits for them, and re-layouts: 0.53 us -> none  [the longest x2 0.38 us: on_device_chain(): prefix.reshape(held_rows, 2, chips, 2 * depth).transpose(2, 0, 1, 3)]
    unnamed x12 -> x9, local copies, waits for them, and re-layouts: 3.29 us -> 2.98 us
where the time goes in v4:
time: 44.2 us; the launch traced here: 44 us
  Pallas kernels  39.7 us (90%)
  local copies, waits for them, and re-layouts  3.65 us (8%)
  other arithmetic  0.6 us (1%)
    pallas_call x1, Pallas kernels, on_device_chain(): pl.pallas_call(lambda *refs: chain_kernel(sizes, *refs), name='chain', ou...  39.7 us
    unnamed x9, local copies, waits for them, and re-layouts  2.98 us

profile of v4, /device:TPU:0, one launch (start us, length us, event | category | flops | bytes accessed | tf_op | source)
XLA Modules:
  0.0 44.0 jit_solution(6835302940785427876)
XLA Ops:
  0.0 0.0 copy-start
  0.0 0.7 %copy-done = s32[8,3]{0,1:T(4,128)S(1)} copy-done((s32[8,3]{0,1:T(4,128)S(1)}, s32[8,3]{0,1:T(4,128)}, u32[]{:S(2)}) %copy-start) | copy-done | bytes 120
  0.7 0.0 copy-start.1
  0.7 0.1 copy.10
  0.8 0.6 %copy-done.1 = s32[8,3]{0,1:T(4,128)S(1)} copy-done((s32[8,3]{0,1:T(4,128)S(1)}, s32[8,3]{0,1:T(4,128)}, u32[]{:S(2)}) %copy-start.1) | copy-done | bytes 120
  1.4 0.1 copy.9
  1.4 0.0 copy-start.2
  1.4 0.6 %multiply_add_fusion.refs_1_ = s32[8,3]{1,0:T(8,128)} fusion(s32[8,3]{1,0:T(8,128)S(1)} %copy.10, s32[8,3]{1,0:T(8,128)S(1)} %copy.9), kind=kLoop, calls=%fused_computation | loop fusion | flops 48 | bytes 288 | tf_op jit(solution)/shard_map/add | solution.py:437
  2.0 0.1 copy-done.2
  2.1 0.7 %copy.11.refs_2_ = s32[8,1]{1,0:T(8,128)} copy(s32[8,1]{0,1:T(1,128)S(1)} %bitcast.11) | data formatting | bytes 64 | tf_op jit(solution)/shard_map/broadcast_in_dim | solution.py:438
  2.8 39.7 %chain.1 = f32[128,128]{1,0:T(8,128)} custom-call(bf16[64,1024]{1,0:T(8,128)(2,1)} %bitcast.9, s32[8,3]{1,0:T(8,128)} %multiply_add_fusion.refs_1_, s32[8,1]{1,0:T(8,128)} %copy.11.refs_2_, s32[8,12]{1,0:T(8,128)} %refs_3_.1, bf16[4,2,32,512]{3,2,1,0:T(8,128)(2,1)} %refs_4_.1, bf16[2,512,512]{2,1,0:T(8,128)(2,1)} %bitcast.7, bf16[128,512]{1,0:T(8,128)(2,1)} %bitcast.10), custom_call_target="tpu_custom_call" | custom-call | tf_op jit(solution)/shard_map/chain/pallas_call | solution.py:445
  42.5 1.5 %copy.13 = f32[8,16,128]{2,1,0:T(8,128)} copy(f32[8,16,128]{2,1,0:T(8,128)} %bitcast.8) | data formatting | bytes 131072
Async XLA Ops:
  0.0 0.7 %copy-start = (s32[8,3]{0,1:T(4,128)S(1)}, s32[8,3]{0,1:T(4,128)}, u32[]{:S(2)}) copy-start(s32[8,3]{0,1:T(4,128)} %param.10) | copy-start | bytes 292
  0.7 0.7 %copy-start.1 = (s32[8,3]{0,1:T(4,128)S(1)}, s32[8,3]{0,1:T(4,128)}, u32[]{:S(2)}) copy-start(s32[8,3]{0,1:T(4,128)} %param.11) | copy-start | bytes 292
  1.4 0.7 %copy-start.2 = (s32[8]{0:T(128)S(1)}, s32[8]{0:T(128)}, u32[]{:S(2)}) copy-start(s32[8]{0:T(128)} %param.12) | copy-start | bytes 100
